TPU v7x, 32 devices: a whole 2x2x4 slice. The times are simulated.
32 devices in a mesh: dp: 4 (over y, x), tensor: 8 (over z, core).
Axes of the slice: x: 2, y: 2, z: 4, core: 2. Of those that a mesh axis runs over, the one named last changes fastest.
Arguments:
- tokens: bfloat16 [2, 6144, 2048], P(None, ('dp', 'tensor')), may hold values from -6 to 6
- cotangent: bfloat16 [2, 6144, 2048], P(None, ('dp', 'tensor')), may hold values from -6 to 6
- lengths: int32 [2, 4, 6], P(None, 'dp'), may hold values from 1 to 1024, 1536 in all within a row
- places: int32 [2, 4, 1536], P(None, 'dp'), may hold values from 0 to 1535, each once within a row
- owners: int32 [4, 4], replicated, may hold values from 0 to 3, each once within a row
- qkv_weight: float32 [3, 2048, 2048], P(None, 'dp', 'tensor'), may hold values from -0.1875 to 0.1875
- qkv_first: float32 [3, 2048, 2048], P(None, 'dp', 'tensor'), may hold values from -1280 to 1280
- qkv_second: float32 [3, 2048, 2048], P(None, 'dp', 'tensor'), may hold values from 49152 to 196608
- out_weight: float32 [2048, 2048], P('tensor', 'dp'), may hold values from -0.375 to 0.375
- out_first: float32 [2048, 2048], P('tensor', 'dp'), may hold values from -320 to 320
- out_second: float32 [2048, 2048], P('tensor', 'dp'), may hold values from 3072 to 12288
- proj_weight: float32 [2, 2048, 8192], P(None, 'dp', 'tensor'), may hold values from -0.125 to 0.125
- proj_first: float32 [2, 2048, 8192], P(None, 'dp', 'tensor'), may hold values from -192 to 192
- proj_second: float32 [2, 2048, 8192], P(None, 'dp', 'tensor'), may hold values from 1105.92 to 4423.68
- down_weight: float32 [8192, 2048], P('tensor', 'dp'), may hold values from -0.0625 to 0.0625
- down_first: float32 [8192, 2048], P('tensor', 'dp'), may hold values from -384 to 384
- down_second: float32 [8192, 2048], P('tensor', 'dp'), may hold values from 4423.68 to 17694.72
Outputs:
- output: bfloat16 [2, 6144, 2048], P(None, ('dp', 'tensor'))
- input_grad: float32 [2, 6144, 2048], P(None, ('dp', 'tensor'))
- qkv_grad: float32 [3, 2048, 2048], P(None, 'dp', 'tensor')
- qkv_first_next: float32 [3, 2048, 2048], P(None, 'dp', 'tensor')
- qkv_second_next: float32 [3, 2048, 2048], P(None, 'dp', 'tensor')
- qkv_master: float32 [3, 2048, 2048], P(None, 'dp', 'tensor')
- out_grad: float32 [2048, 2048], P('tensor', 'dp')
- out_first_next: float32 [2048, 2048], P('tensor', 'dp')
- out_second_next: float32 [2048, 2048], P('tensor', 'dp')
- out_master: float32 [2048, 2048], P('tensor', 'dp')
- proj_grad: float32 [2, 2048, 8192], P(None, 'dp', 'tensor')
- proj_first_next: float32 [2, 2048, 8192], P(None, 'dp', 'tensor')
- proj_second_next: float32 [2, 2048, 8192], P(None, 'dp', 'tensor')
- proj_master: float32 [2, 2048, 8192], P(None, 'dp', 'tensor')
- down_grad: float32 [8192, 2048], P('tensor', 'dp')
- down_first_next: float32 [8192, 2048], P('tensor', 'dp')
- down_second_next: float32 [8192, 2048], P('tensor', 'dp')
- down_master: float32 [8192, 2048], P('tensor', 'dp')
Inputs may be any that keep to these rules, and one draw needn't show every extreme that they name: Each row of 6 lengths sums to 1536 and its largest is exactly 1024. `places`: each row names every place of its group once. `owners`: each row names every block once.
All inputs are finite; a program needn't handle non-finite values.
Results may differ from a plain program's by a relative error of at most 0.02.
Values may be sent and summed in bfloat16 or wider, within the bound.
No kernel may reach another device: no remote copies, remote signals or barrier semaphores. Data moves between devices by JAX's collectives and lax.ppermute only.
A program may use at most 320 MiB of HBM per device.

v0:
```python
import math
import jax
import jax.numpy as jnp
from jax import lax
from jax.sharding import PartitionSpec as P

HD = 128
RATES = (0.03, 0.06, 0.02, 0.01)


def inverse_order(order):
    count = order.shape[0]
    return jnp.zeros((count,), jnp.int32).at[order].set(jnp.arange(count, dtype=jnp.int32))


def reorder_blocks(weight, order):
    shape = weight.shape
    split = shape[:1] + (order.shape[0], shape[1] // order.shape[0]) + shape[2:]
    return jnp.take(weight.reshape(split), order, axis=1).reshape(shape)


def normalize(values):
    center = values - jnp.mean(values, axis=-1, keepdims=True)
    scale = lax.rsqrt(jnp.mean(center * center, axis=-1, keepdims=True) + 1e-05)
    return (center * scale, scale)


def normalize_back(normed, scale, grad):
    return scale * (
        grad
        - jnp.mean(grad, axis=-1, keepdims=True)
        - normed * jnp.mean(grad * normed, axis=-1, keepdims=True)
    )


def rotate(values, cosine, sine):
    half = values.shape[-1] // 2
    first = values[..., :half]
    second = values[..., half:]
    return jnp.concatenate(
        [first * cosine - second * sine, second * cosine + first * sine], axis=-1
    )


def rotate_back(grad, cosine, sine):
    half = grad.shape[-1] // 2
    first = grad[..., :half]
    second = grad[..., half:]
    return jnp.concatenate(
        [first * cosine + second * sine, second * cosine - first * sine], axis=-1
    )


def layout(lengths, count, head_size):
    place = jnp.arange(count, dtype=jnp.int32)
    ends = jnp.cumsum(lengths)
    starts = ends - lengths
    segment = jnp.sum((place[:, None] >= ends[None, :]).astype(jnp.int32), axis=1)
    begin = jnp.max(jnp.where(starts[None, :] <= place[:, None], starts[None, :], 0), axis=1)
    position = (place - begin).astype(jnp.float32)
    half = head_size // 2
    freq = jnp.exp(jnp.arange(half, dtype=jnp.float32) * (-2.0 * math.log(10000.0) / head_size))
    angle = position[:, None] * freq[None, :]
    return (segment, place, jnp.cos(angle), jnp.sin(angle))


def block_scores(query_block, keys, segment, place, start, width):
    finish = start + width
    scores = jnp.einsum(
        "hqd,hkd->hqk", query_block, keys[:, :finish], preferred_element_type=jnp.float32
    ) * keys.shape[-1] ** (-0.5)
    allowed = (segment[start:finish][:, None] == segment[None, :finish]) & (
        place[None, :finish] <= place[start:finish][:, None]
    )
    return jnp.where(allowed[None], scores, -1e30)


def gather_normed(rows):
    return lax.all_gather(rows, "tensor", axis=0, tiled=True)


def gather_grads(rows):
    return lax.all_gather(rows, "tensor", axis=0, tiled=True)


def sum_branch(partial_rows):
    return lax.psum_scatter(
        partial_rows.astype(jnp.bfloat16), "tensor", scatter_dimension=0, tiled=True
    ).astype(jnp.float32)


def sum_inputs(partial_rows):
    return lax.psum_scatter(
        partial_rows.astype(jnp.bfloat16), "tensor", scatter_dimension=0, tiled=True
    ).astype(jnp.float32)


def reduce_owned(terms, owners):
    return (
        lax.psum_scatter(
            reorder_blocks(terms[0], owners[0]).astype(jnp.bfloat16),
            "dp",
            scatter_dimension=1,
            tiled=True,
        ).astype(jnp.float32),
        lax.psum_scatter(
            reorder_blocks(terms[1], owners[1]).astype(jnp.bfloat16),
            "dp",
            scatter_dimension=1,
            tiled=True,
        ).astype(jnp.float32),
        lax.psum_scatter(
            reorder_blocks(terms[2], owners[2]).astype(jnp.bfloat16),
            "dp",
            scatter_dimension=1,
            tiled=True,
        ).astype(jnp.float32),
        lax.psum_scatter(
            reorder_blocks(terms[3], owners[3]).astype(jnp.bfloat16),
            "dp",
            scatter_dimension=1,
            tiled=True,
        ).astype(jnp.float32),
    )


def adamw(master, first, second, grad, rate):
    first_next = 0.5 * first + 0.5 * grad
    second_next = 0.5 * second + 0.5 * grad * grad
    master_next = master - rate * (first_next / (jnp.sqrt(second_next) + 1e-08) + 0.1 * master)
    return (grad, first_next, second_next, master_next)


def body(
    tokens,
    cotangent,
    lengths,
    places,
    owners,
    qkv_weight,
    qkv_first,
    qkv_second,
    out_weight,
    out_first,
    out_second,
    proj_weight,
    proj_first,
    proj_second,
    down_weight,
    down_first,
    down_second,
):
    fetched = (
        lax.all_gather(qkv_weight.astype(jnp.bfloat16), "dp", axis=1, tiled=True),
        lax.all_gather(out_weight.astype(jnp.bfloat16), "dp", axis=1, tiled=True),
        lax.all_gather(proj_weight.astype(jnp.bfloat16), "dp", axis=1, tiled=True),
        lax.all_gather(down_weight.astype(jnp.bfloat16), "dp", axis=1, tiled=True),
    )
    w_qkv = reorder_blocks(fetched[0], inverse_order(owners[0]))
    w_out = reorder_blocks(fetched[1], inverse_order(owners[1]))
    w_proj = reorder_blocks(fetched[2], inverse_order(owners[2]))
    w_down = reorder_blocks(fetched[3], inverse_order(owners[3]))
    local_cols = w_qkv.shape[2]
    local_heads = local_cols // HD
    group_rows = places.shape[2]
    width = min(512, group_rows)
    scale = HD ** (-0.5)
    logical = (
        jnp.zeros(w_qkv.shape, jnp.float32),
        jnp.zeros(w_out.shape, jnp.float32),
        jnp.zeros(w_proj.shape, jnp.float32),
        jnp.zeros(w_down.shape, jnp.float32),
    )
    owned = (
        jnp.zeros(qkv_weight.shape, jnp.float32),
        jnp.zeros(out_weight.shape, jnp.float32),
        jnp.zeros(proj_weight.shape, jnp.float32),
        jnp.zeros(down_weight.shape, jnp.float32),
    )
    outputs = []
    input_grads = []
    for micro_batch in range(tokens.shape[0]):
        order = places[micro_batch, 0]
        back = inverse_order(order)
        segment, place, cosine, sine = layout(lengths[micro_batch, 0], group_rows, HD)
        rows_in = tokens[micro_batch].astype(jnp.float32)
        normed_one, scale_one = normalize(rows_in)
        rows_a = gather_normed(normed_one.astype(jnp.bfloat16))[order]
        joined = jnp.einsum("td,sdc->stc", rows_a, w_qkv, preferred_element_type=jnp.float32)
        heads = joined.reshape(3, group_rows, local_heads, HD).transpose(0, 2, 1, 3)
        query = rotate(heads[0], cosine, sine).astype(jnp.bfloat16)
        keys = rotate(heads[1], cosine, sine).astype(jnp.bfloat16)
        values = heads[2].astype(jnp.bfloat16)
        pieces = []
        lse_list = []
        for start in range(0, group_rows, width):
            finish = start + width
            scores = block_scores(query[:, start:finish], keys, segment, place, start, width)
            top = jnp.max(scores, axis=-1, keepdims=True)
            expo = jnp.exp(scores - top)
            total = jnp.sum(expo, axis=-1, keepdims=True)
            probs = expo / total
            lse_list.append(top + jnp.log(total))
            pieces.append(
                jnp.einsum(
                    "hqk,hkd->hqd",
                    probs.astype(jnp.bfloat16),
                    values[:, :finish],
                    preferred_element_type=jnp.float32,
                )
            )
        attended = jnp.concatenate(pieces, axis=1).astype(jnp.bfloat16)
        attn_rows = attended.transpose(1, 0, 2).reshape(group_rows, local_cols)
        branch_one = sum_branch(jnp.dot(attn_rows, w_out, preferred_element_type=jnp.float32)[back])
        middle = rows_in + branch_one
        normed_two, scale_two = normalize(middle)
        rows_b = gather_normed(normed_two.astype(jnp.bfloat16))
        gate_up = jnp.einsum("td,sdf->stf", rows_b, w_proj, preferred_element_type=jnp.float32)
        sigma = jax.nn.sigmoid(gate_up[0])
        activated = gate_up[0] * sigma
        hidden = (activated * gate_up[1]).astype(jnp.bfloat16)
        branch_two = sum_branch(jnp.dot(hidden, w_down, preferred_element_type=jnp.float32))
        outputs.append((middle + branch_two).astype(jnp.bfloat16))
        grad_out = cotangent[micro_batch].astype(jnp.float32)
        grads_two = gather_grads(grad_out.astype(jnp.bfloat16))
        term_down = jnp.einsum("tf,td->fd", hidden, grads_two, preferred_element_type=jnp.float32)
        grad_hidden = jnp.einsum("td,fd->tf", grads_two, w_down, preferred_element_type=jnp.float32)
        grad_gate = grad_hidden * gate_up[1] * sigma * (1.0 + gate_up[0] * (1.0 - sigma))
        grad_up = grad_hidden * activated
        grad_gate_up = jnp.stack([grad_gate, grad_up]).astype(jnp.bfloat16)
        term_proj = jnp.einsum(
            "td,stf->sdf", rows_b, grad_gate_up, preferred_element_type=jnp.float32
        )
        grad_normed_two = sum_inputs(
            jnp.einsum("stf,sdf->td", grad_gate_up, w_proj, preferred_element_type=jnp.float32)
        )
        grad_middle = grad_out + normalize_back(normed_two, scale_two, grad_normed_two)
        grads_one = gather_grads(grad_middle.astype(jnp.bfloat16))[order]
        term_out = jnp.einsum("tc,td->cd", attn_rows, grads_one, preferred_element_type=jnp.float32)
        grad_attn = jnp.einsum(
            "td,cd->tc", grads_one, w_out, preferred_element_type=jnp.float32
        ).astype(jnp.bfloat16)
        grad_heads = grad_attn.reshape(group_rows, local_heads, HD).transpose(1, 0, 2)
        grad_query_list = []
        grad_keys = jnp.zeros(keys.shape, jnp.float32)
        grad_values = jnp.zeros(values.shape, jnp.float32)
        for number, start in enumerate(range(0, group_rows, width)):
            finish = start + width
            query_block = query[:, start:finish]
            grad_block = grad_heads[:, start:finish]
            scores = block_scores(query_block, keys, segment, place, start, width)
            probs = jnp.exp(scores - lse_list[number])
            grad_probs = jnp.einsum(
                "hqd,hkd->hqk", grad_block, values[:, :finish], preferred_element_type=jnp.float32
            )
            delta = jnp.sum(grad_probs * probs, axis=-1, keepdims=True)
            grad_scores = (probs * (grad_probs - delta)).astype(jnp.bfloat16)
            grad_query_list.append(
                jnp.einsum(
                    "hqk,hkd->hqd",
                    grad_scores,
                    keys[:, :finish],
                    preferred_element_type=jnp.float32,
                )
                * scale
            )
            grad_keys = grad_keys.at[:, :finish].add(
                jnp.einsum(
                    "hqk,hqd->hkd", grad_scores, query_block, preferred_element_type=jnp.float32
                )
                * scale
            )
            grad_values = grad_values.at[:, :finish].add(
                jnp.einsum(
                    "hqk,hqd->hkd",
                    probs.astype(jnp.bfloat16),
                    grad_block,
                    preferred_element_type=jnp.float32,
                )
            )
        grad_query = rotate_back(jnp.concatenate(grad_query_list, axis=1), cosine, sine)
        grad_keys = rotate_back(grad_keys, cosine, sine)
        grad_joined = jnp.stack([grad_query, grad_keys, grad_values]).astype(jnp.bfloat16)
        grad_joined = grad_joined.transpose(0, 2, 1, 3).reshape(3, group_rows, local_cols)
        term_qkv = jnp.einsum(
            "td,stc->sdc", rows_a, grad_joined, preferred_element_type=jnp.float32
        )
        grad_normed_one = sum_inputs(
            jnp.einsum("stc,sdc->td", grad_joined, w_qkv, preferred_element_type=jnp.float32)[back]
        )
        input_grads.append(grad_middle + normalize_back(normed_one, scale_one, grad_normed_one))
        terms = (term_qkv, term_out, term_proj, term_down)
        logical = tuple((running + current for running, current in zip(logical, terms)))
    owned = reduce_owned(logical, owners)
    qkv_new = adamw(qkv_weight, qkv_first, qkv_second, owned[0], RATES[0])
    out_new = adamw(out_weight, out_first, out_second, owned[1], RATES[1])
    proj_new = adamw(proj_weight, proj_first, proj_second, owned[2], RATES[2])
    down_new = adamw(down_weight, down_first, down_second, owned[3], RATES[3])
    return (
        jnp.stack(outputs),
        jnp.stack(input_grads),
        qkv_new[0],
        qkv_new[1],
        qkv_new[2],
        qkv_new[3],
        out_new[0],
        out_new[1],
        out_new[2],
        out_new[3],
        proj_new[0],
        proj_new[1],
        proj_new[2],
        proj_new[3],
        down_new[0],
        down_new[1],
        down_new[2],
        down_new[3],
    )


def solution(mesh):
    placed = (
        P(None, ("dp", "tensor"), None),
        P(None, ("dp", "tensor"), None),
        P(None, "dp", None),
        P(None, "dp", None),
        P(),
        P(None, "dp", "tensor"),
        P(None, "dp", "tensor"),
        P(None, "dp", "tensor"),
        P("tensor", "dp"),
        P("tensor", "dp"),
        P("tensor", "dp"),
        P(None, "dp", "tensor"),
        P(None, "dp", "tensor"),
        P(None, "dp", "tensor"),
        P("tensor", "dp"),
        P("tensor", "dp"),
        P("tensor", "dp"),
    )
    return jax.shard_map(
        body,
        mesh=mesh,
        in_specs=placed,
        out_specs=(
            P(None, ("dp", "tensor"), None),
            P(None, ("dp", "tensor"), None),
            P(None, "dp", "tensor"),
            P(None, "dp", "tensor"),
            P(None, "dp", "tensor"),
            P(None, "dp", "tensor"),
            P("tensor", "dp"),
            P("tensor", "dp"),
            P("tensor", "dp"),
            P("tensor", "dp"),
            P(None, "dp", "tensor"),
            P(None, "dp", "tensor"),
            P(None, "dp", "tensor"),
            P(None, "dp", "tensor"),
            P("tensor", "dp"),
            P("tensor", "dp"),
            P("tensor", "dp"),
            P("tensor", "dp"),
        ),
        check_vma=False,
    )
```

profile of v0, /device:TPU:0, one launch (start us, length us, event | category | flops | bytes accessed | tf_op | source)
XLA Modules:
  0.0 1725.9 jit_solution(1794120397904735243)
XLA Ops:
  48.3 38.6 %all-gather.15.cloned.1.call-done = bf16[3,2048,256]{2,1,0:T(8,128)(2,1)} async-done(((bf16[3,512,256]{2,1,0:T(8,128)(2,1)}), bf16[3,2048,256]{2,1,0:T(8,128)(2,1)}) %all-gather.15.cloned.1.call-update) | async-done | bytes 3145744 | tf_op jit(solution)/shard_map/all_gather | solution.py:154
  95.4 58.4 %all-gather.17.cloned.1.call-done = bf16[1536,2048]{1,0:T(8,128)(2,1)} async-done(((bf16[192,2048]{1,0:T(8,128)(2,1)}), bf16[1536,2048]{1,0:T(8,128)(2,1)}) %all-gather.17.cloned.1.call-update) | async-done | bytes 6291472 | tf_op jit(solution)/shard_map/all_gather | solution.py:79
  153.9 16.3 gather_fusion.1
  213.5 16.3 gather_fusion.3
  236.9 61.5 %reduce-scatter.13.cloned.1.call-done = bf16[192,2048]{1,0:T(8,128)(2,1)} async-done(((bf16[1536,2048]{1,0:T(8,128)(2,1)}), bf16[192,2048]{1,0:T(8,128)(2,1)}) %reduce-scatter.13.cloned.1.call-update) | async-done | bytes 786448 | tf_op jit(solution)/shard_map/reduce_scatter | solution.py:87
  306.9 44.8 %all-gather.25.cloned.1.call-done = bf16[1024,2048]{1,0:T(8,128)(2,1)} async-done(((bf16[1024,512]{1,0:T(8,128)(2,1)}), bf16[1024,2048]{1,0:T(8,128)(2,1)}) %all-gather.25.cloned.1.call-update) | async-done | bytes 4194320 | tf_op jit(solution)/shard_map/all_gather | solution.py:157
  368.4 73.0 %all-gather.21.cloned.1.call-done = bf16[2,2048,1024]{2,1,0:T(8,128)(2,1)} async-done(((bf16[2,512,1024]{2,1,0:T(8,128)(2,1)}), bf16[2,2048,1024]{2,1,0:T(8,128)(2,1)}) %all-gather.21.cloned.1.call-update) | async-done | bytes 8388624 | tf_op jit(solution)/shard_map/all_gather | solution.py:156
  480.8 27.6 %all-gather.23.cloned.1.call-done = bf16[1536,2048]{1,0:T(8,128)(2,1)} async-done(((bf16[192,2048]{1,0:T(8,128)(2,1)}), bf16[1536,2048]{1,0:T(8,128)(2,1)}) %all-gather.23.cloned.1.call-update) | async-done | bytes 6291472 | tf_op jit(solution)/shard_map/all_gather | solution.py:79
  508.3 19.2 %convolution_bitcast_fusion.3 = f32[2,1536,1024]{1,2,0:T(8,128)} fusion(bf16[2,2048,1024]{2,1,0:T(8,128)(2,1)} %bitcast_select_fusion.1, bf16[1536,2048]{1,0:T(8,128)(2,1)} %all-gather.23.cloned.1.call-done), kind=kOutput, calls=%fused_computation.38 | convolution fusion | flops 12884901888 | bytes 27262976 | tf_op jit(solution)/shard_map/td,sdf->stf/dot_general | solution.py:218
  546.3 27.0 %all-gather.35.cloned.1.call-done = bf16[1,1536,2048]{2,1,0:T(8,128)(2,1)} async-done(((bf16[1,192,2048]{2,1,0:T(8,128)(2,1)}), bf16[1,1536,2048]{2,1,0:T(8,128)(2,1)}) %all-gather.35.cloned.1.call-update) | async-done | bytes 6291472 | tf_op jit(solution)/shard_map/all_gather | solution.py:83
  590.9 17.7 %bitcast_convert_fusion.1 = bf16[1536,2048]{1,0:T(8,128)(2,1)} fusion(bf16[2,2048,1024]{2,1,0:T(8,128)(2,1)} %bitcast_select_fusion.1, bf16[1,1536,1024]{1,2,0:T(8,128)(2,1)S(1)} %get-tuple-element.266, bf16[1,1536,1024]{1,2,0:T(8,128)(2,1)S(1)} %get-tuple-element.265), kind=kOutput, calls=%fused_computation.29 | convolution fusion | flops 12891193344 | bytes 20971520 | tf_op jit(solution)/shard_map/stf,sdf->td/dot_general | solution.py:235
  609.2 34.9 %reduce-scatter.15.cloned.1.call-done = bf16[192,2048]{1,0:T(8,128)(2,1)} async-done(((bf16[1536,2048]{1,0:T(8,128)(2,1)}), bf16[192,2048]{1,0:T(8,128)(2,1)}) %reduce-scatter.15.cloned.1.call-update) | async-done | bytes 786448 | tf_op jit(solution)/shard_map/reduce_scatter | solution.py:87
  644.1 70.4 %reduce-scatter.21.cloned.1.call-done = bf16[192,2048]{1,0:T(8,128)(2,1)} async-done(((bf16[1536,2048]{1,0:T(8,128)(2,1)}), bf16[192,2048]{1,0:T(8,128)(2,1)}) %reduce-scatter.21.cloned.1.call-update) | async-done | bytes 786448 | tf_op jit(solution)/shard_map/reduce_scatter | solution.py:93
  727.3 56.4 %all-gather.27.cloned.1.call-done = bf16[1536,2048]{1,0:T(8,128)(2,1)} async-done(((bf16[192,2048]{1,0:T(8,128)(2,1)}), bf16[1536,2048]{1,0:T(8,128)(2,1)}) %all-gather.27.cloned.1.call-update) | async-done | bytes 6291472 | tf_op jit(solution)/shard_map/all_gather | solution.py:79
  783.7 16.3 gather_fusion.5
  838.1 16.3 gather_fusion.6
  857.0 17.1 gather_fusion.7
  916.7 16.4 gather_fusion.8
  933.2 68.0 %reduce-scatter.23.cloned.1.call-done = bf16[192,2048]{1,0:T(8,128)(2,1)} async-done(((bf16[1536,2048]{1,0:T(8,128)(2,1)}), bf16[192,2048]{1,0:T(8,128)(2,1)}) %reduce-scatter.23.cloned.1.call-update) | async-done | bytes 786448 | tf_op jit(solution)/shard_map/reduce_scatter | solution.py:93
  1006.1 62.7 %all-gather.29.cloned.1.call-done = bf16[1536,2048]{1,0:T(8,128)(2,1)} async-done(((bf16[192,2048]{1,0:T(8,128)(2,1)}), bf16[1536,2048]{1,0:T(8,128)(2,1)}) %all-gather.29.cloned.1.call-update) | async-done | bytes 6291472 | tf_op jit(solution)/shard_map/all_gather | solution.py:79
  1068.8 19.2 %convolution_bitcast_fusion.2 = f32[2,1536,1024]{1,2,0:T(8,128)} fusion(bf16[2,2048,1024]{2,1,0:T(8,128)(2,1)} %bitcast_select_fusion.1, bf16[1536,2048]{1,0:T(8,128)(2,1)} %all-gather.29.cloned.1.call-done), kind=kOutput, calls=%fused_computation.37 | convolution fusion | flops 12884901888 | bytes 27262976 | tf_op jit(solution)/shard_map/td,sdf->stf/dot_general | solution.py:218
  1088.0 46.2 %all-gather.37.cloned.1.call-done = bf16[1,1536,2048]{2,1,0:T(8,128)(2,1)} async-done(((bf16[1,192,2048]{2,1,0:T(8,128)(2,1)}), bf16[1,1536,2048]{2,1,0:T(8,128)(2,1)}) %all-gather.37.cloned.1.call-update) | async-done | bytes 6291472 | tf_op jit(solution)/shard_map/all_gather | solution.py:83
  1134.2 15.1 fusion.72
  1151.9 17.8 %bitcast_convert_fusion = bf16[1536,2048]{1,0:T(8,128)(2,1)} fusion(bf16[2,2048,1024]{2,1,0:T(8,128)(2,1)} %bitcast_select_fusion.1, bf16[1,1536,1024]{1,2,0:T(8,128)(2,1)S(1)} %get-tuple-element.264, bf16[1,1536,1024]{1,2,0:T(8,128)(2,1)S(1)} %get-tuple-element.263), kind=kOutput, calls=%fused_computation.28 | convolution fusion | flops 12891193344 | bytes 20971520 | tf_op jit(solution)/shard_map/stf,sdf->td/dot_general | solution.py:235
  1169.8 15.1 convolution_convert_fusion
  1185.4 52.9 %reduce-scatter.25.cloned.1.call-done = bf16[192,2048]{1,0:T(8,128)(2,1)} async-done(((bf16[1536,2048]{1,0:T(8,128)(2,1)}), bf16[192,2048]{1,0:T(8,128)(2,1)}) %reduce-scatter.25.cloned.1.call-update) | async-done | bytes 786448 | tf_op jit(solution)/shard_map/reduce_scatter | solution.py:93
  1240.1 68.5 %reduce-scatter.19.cloned.1.call-done = bf16[192,2048]{1,0:T(8,128)(2,1)} async-done(((bf16[1536,2048]{1,0:T(8,128)(2,1)}), bf16[192,2048]{1,0:T(8,128)(2,1)}) %reduce-scatter.19.cloned.1.call-update) | async-done | bytes 786448 | tf_op jit(solution)/shard_map/reduce_scatter | solution.py:87
  1363.2 19.6 %fusion.34 = f32[2,1024,2048]{2,1,0:T(8,128)} fusion(bf16[1536,2048]{1,0:T(8,128)(2,1)} %all-gather.23.cloned.1.call-done, bf16[1,1536,1024]{1,2,0:T(8,128)(2,1)} %copy-done.149, bf16[1,1536,1024]{1,2,0:T(8,128)(2,1)S(1)} %copy-done.148), kind=kOutput, calls=%fused_computation.87 | convolution fusion | flops 12888047616 | bytes 29360128 | tf_op jit(solution)/shard_map/td,stf->sdf/dot_general | solution.py:231
  1382.8 22.3 %add_bitcast_fusion = bf16[2,2048,1024]{1,2,0:T(8,128)(2,1)} fusion(f32[2,1024,2048]{2,1,0:T(8,128)} %fusion.34, bf16[1536,2048]{1,0:T(8,128)(2,1)} %all-gather.29.cloned.1.call-done, bf16[1,1536,1024]{1,2,0:T(8,128)(2,1)} %copy-done.151, bf16[1,1536,1024]{1,2,0:T(8,128)(2,1)} %copy-done.150), kind=kOutput, calls=%fused_computation.27 | convolution fusion | flops 12896436224 | bytes 37748736 | tf_op jit(solution)/shard_map/td,stf->sdf/dot_general | solution.py:231
  1483.9 16.4 gather_fusion.9
  1585.1 16.5 gather_fusion.10
  1646.0 66.3 %reduce-scatter.27.cloned.1.call-done = bf16[192,2048]{1,0:T(8,128)(2,1)} async-done(((bf16[1536,2048]{1,0:T(8,128)(2,1)}), bf16[192,2048]{1,0:T(8,128)(2,1)}) %reduce-scatter.27.cloned.1.call-update) | async-done | bytes 786448 | tf_op jit(solution)/shard_map/reduce_scatter | solution.py:93
  (638 shorter events, 574.0 us)
Async XLA Ops:
  7.2 33.4 %all-gather.19.cloned.1.call-start = ((), (), s32[]{:S(2)}) async-start(), calls=%async_computation.14 | async-start | bytes 1310720 | tf_op jit(solution)/shard_map/all_gather | solution.py:155
  11.2 75.7 %all-gather.15.cloned.1.call-start = ((), (), s32[]{:S(2)}) async-start(), calls=%async_computation.12 | async-start | bytes 3932160 | tf_op jit(solution)/shard_map/all_gather | solution.py:154
  12.3 141.6 %all-gather.17.cloned.1.call-start = ((), (), s32[]{:S(2)}) async-start(), calls=%async_computation.13 | async-start | bytes 7077888 | tf_op jit(solution)/shard_map/all_gather | solution.py:79
  15.6 282.8 %reduce-scatter.13.cloned.1.call-start = ((), (), s32[]{:S(2)}) async-start(), calls=%async_computation.15 | async-start | bytes 7077888 | tf_op jit(solution)/shard_map/reduce_scatter | solution.py:87
  16.1 289.5 %copy-start.143 = (s32[4]{0:T(128)}, s32[4]{0:T(128)S(1)}, u32[]{:S(2)}) copy-start(s32[4]{0:T(128)S(1)} %get-tuple-element.328) | copy-start | bytes 52
  25.3 128.5 %copy-start.88 = (s32[2048]{0:T(1024)}, s32[2048]{0:T(1024)S(1)}, u32[]{:S(2)}) copy-start(s32[2048]{0:T(1024)S(1)} %pad_clamp_fusion.3) | copy-start | bytes 24580
  25.4 188.2 %copy-start.86 = (s32[2048]{0:T(1024)}, s32[2048]{0:T(1024)S(1)}, u32[]{:S(2)}) copy-start(s32[2048]{0:T(1024)S(1)} %pad_clamp_fusion.2) | copy-start | bytes 24580
  35.7 154.5 %copy-start.40 = (f32[1536,64]{1,0:T(8,128)}, f32[1536,64]{1,0:T(8,128)S(1)}, u32[]{:S(2)}) copy-start(f32[1536,64]{1,0:T(8,128)S(1)} %get-tuple-element.334) | copy-start | bytes 1179652
  48.3 160.6 %copy-start.31 = (bf16[256,4,512]{0,2,1:T(8,128)(2,1)}, bf16[256,4,512]{0,2,1:T(8,128)(2,1)S(1)}, u32[]{:S(2)}) copy-start(bf16[256,4,512]{0,2,1:T(8,128)(2,1)S(1)} %copy.218) | copy-start | bytes 3145732
  229.9 121.7 %all-gather.25.cloned.1.call-start = ((), (), s32[]{:S(2)}) async-start(), calls=%async_computation.18 | async-start | bytes 5242880 | tf_op jit(solution)/shard_map/all_gather | solution.py:157
  232.7 208.7 %all-gather.21.cloned.1.call-start = ((), (), s32[]{:S(2)}) async-start(), calls=%async_computation.16 | async-start | bytes 10485760 | tf_op jit(solution)/shard_map/all_gather | solution.py:156
  236.9 271.4 %all-gather.23.cloned.1.call-start = ((), (), s32[]{:S(2)}) async-start(), calls=%async_computation.17 | async-start | bytes 7077888 | tf_op jit(solution)/shard_map/all_gather | solution.py:79
  302.7 270.7 %all-gather.35.cloned.1.call-start = ((), (), s32[]{:S(2)}) async-start(), calls=%async_computation.34 | async-start | bytes 7077888 | tf_op jit(solution)/shard_map/all_gather | solution.py:83
  305.5 338.6 %reduce-scatter.15.cloned.1.call-start = ((), (), s32[]{:S(2)}) async-start(), calls=%async_computation.19 | async-start | bytes 7077888 | tf_op jit(solution)/shard_map/reduce_scatter | solution.py:87
  541.9 172.6 %reduce-scatter.21.cloned.1.call-start = ((), (), s32[]{:S(2)}) async-start(), calls=%async_computation.24 | async-start | bytes 7077888 | tf_op jit(solution)/shard_map/reduce_scatter | solution.py:93
  608.6 175.1 %all-gather.27.cloned.1.call-start = ((), (), s32[]{:S(2)}) async-start(), calls=%async_computation.20 | async-start | bytes 7077888 | tf_op jit(solution)/shard_map/all_gather | solution.py:79
  609.2 111.1 %copy-start.108 = (f32[192]{0:T(256)}, f32[192]{0:T(256)S(1)}, u32[]{:S(2)}) copy-start(f32[192]{0:T(256)S(1)} %broadcast_multiply_fusion.9) | copy-start | bytes 2308
  720.4 136.6 %all-gather.31.cloned.1.call-start = ((), (), s32[]{:S(2)}) async-start(), calls=%async_computation.25 | async-start | bytes 7077888 | tf_op jit(solution)/shard_map/all_gather | solution.py:83
  721.0 212.2 %reduce-scatter.17.cloned.1.call-start = ((), (), s32[]{:S(2)}) async-start(), calls=%async_computation.21 | async-start | bytes 7077888 | tf_op jit(solution)/shard_map/reduce_scatter | solution.py:87
  727.3 110.8 %copy-start.84 = (s32[2048]{0:T(1024)}, s32[2048]{0:T(1024)S(1)}, u32[]{:S(2)}) copy-start(s32[2048]{0:T(1024)S(1)} %pad_clamp_fusion) | copy-start | bytes 24580
  854.5 146.7 %reduce-scatter.23.cloned.1.call-start = ((), (), s32[]{:S(2)}) async-start(), calls=%async_computation.26 | async-start | bytes 7077888 | tf_op jit(solution)/shard_map/reduce_scatter | solution.py:93
  933.1 135.7 %all-gather.29.cloned.1.call-start = ((), (), s32[]{:S(2)}) async-start(), calls=%async_computation.22 | async-start | bytes 7077888 | tf_op jit(solution)/shard_map/all_gather | solution.py:79
  1005.5 128.8 %all-gather.37.cloned.1.call-start = ((), (), s32[]{:S(2)}) async-start(), calls=%async_computation.35 | async-start | bytes 7077888 | tf_op jit(solution)/shard_map/all_gather | solution.py:83
  1006.0 232.2 %reduce-scatter.25.cloned.1.call-start = ((), (), s32[]{:S(2)}) async-start(), calls=%async_computation.27 | async-start | bytes 7077888 | tf_op jit(solution)/shard_map/reduce_scatter | solution.py:93
  1169.8 138.9 %reduce-scatter.19.cloned.1.call-start = ((), (), s32[]{:S(2)}) async-start(), calls=%async_computation.23 | async-start | bytes 7077888 | tf_op jit(solution)/shard_map/reduce_scatter | solution.py:87
  1185.0 299.0 %all-gather.33.cloned.1.call-start = ((), (), s32[]{:S(2)}) async-start(), calls=%async_computation.28 | async-start | bytes 7077888 | tf_op jit(solution)/shard_map/all_gather | solution.py:83
  1312.9 292.0 %reduce-scatter.35.cloned.1.call-start = ((), (), s32[]{:S(2)}) async-start(), calls=%async_computation.33 | async-start | bytes 5242880 | tf_op jit(solution)/shard_map/reduce_scatter | solution.py:118
  1361.3 251.7 %reduce-scatter.33.cloned.1.call-start = ((), (), s32[]{:S(2)}) async-start(), calls=%async_computation.32 | async-start | bytes 10485760 | tf_op jit(solution)/shard_map/reduce_scatter | solution.py:112
  1476.9 146.9 %reduce-scatter.31.cloned.1.call-start = ((), (), s32[]{:S(2)}) async-start(), calls=%async_computation.31 | async-start | bytes 1310720 | tf_op jit(solution)/shard_map/reduce_scatter | solution.py:106
  1546.6 93.8 %reduce-scatter.29.cloned.1.call-start = ((), (), s32[]{:S(2)}) async-start(), calls=%async_computation.30 | async-start | bytes 3932160 | tf_op jit(solution)/shard_map/reduce_scatter | solution.py:100
  1574.2 138.1 %reduce-scatter.27.cloned.1.call-start = ((), (), s32[]{:S(2)}) async-start(), calls=%async_computation.29 | async-start | bytes 7077888 | tf_op jit(solution)/shard_map/reduce_scatter | solution.py:93
  1629.1 84.8 %copy-start.107 = (f32[192]{0:T(256)S(1)}, f32[192]{0:T(256)}, u32[]{:S(2)}) copy-start(f32[192]{0:T(256)} %copy-done.105) | copy-start | bytes 2308
  (150 other events, 1606.2 us)
Sparse Core Ops, SparseCore 0:
  11.4 29.2 all-gather.18
  43.0 43.8 all-gather.14
  89.1 64.6 all-gather.16
  230.0 68.3 reduce-scatter.12
  300.7 50.8 all-gather.24
  353.9 87.4 all-gather.20
  443.6 64.6 all-gather.22
  510.0 63.3 all-gather.34
  575.6 68.3 reduce-scatter.14
  646.2 68.1 reduce-scatter.20
  720.5 63.1 all-gather.26
  785.7 63.3 all-gather.30
  854.5 68.4 reduce-scatter.16
  933.2 67.9 reduce-scatter.22
  1005.6 63.1 all-gather.28
  1070.8 63.3 all-gather.36
  1169.9 68.3 reduce-scatter.24
  1240.4 68.1 reduce-scatter.18
  1313.1 63.1 all-gather.32
  1379.1 51.2 reduce-scatter.34
  1477.0 84.8 reduce-scatter.32
  1565.4 27.9 reduce-scatter.30
  1596.4 43.9 reduce-scatter.28
  1642.5 69.7 reduce-scatter.26
where the time goes:
time: 1730 us
  waiting for transfers between devices  872 us (50%)
  local copies, waits for them, and re-layouts  352 us (20%)
  matrix products  330 us (19%)
  other arithmetic  153 us (9%)
  between operations  17.3 us (1%)
    reduce_scatter x4, waiting for transfers between devices, sum_inputs(): lax.psum_scatter(partial_rows.astype(jnp.bfloat16), 'tensor', scatter_dim...  258 us
    all_gather x4, waiting for transfers between devices, gather_normed(): return lax.all_gather(rows, 'tensor', axis=0, tiled=True)  205 us
    reduce_scatter x4, waiting for transfers between devices, sum_branch(): lax.psum_scatter(partial_rows.astype(jnp.bfloat16), 'tensor', scatter_dim...  165 us
    all_gather x4, waiting for transfers between devices, gather_grads(): return lax.all_gather(rows, 'tensor', axis=0, tiled=True)  73.3 us
    all_gather x1, waiting for transfers between devices, body(): lax.all_gather(proj_weight.astype(jnp.bfloat16), 'dp', axis=1, tiled=True)  73 us
    gather x17, local copies, waits for them, and re-layouts, reorder_blocks(): return jnp.take(weight.reshape(split), order, axis=1).reshape(shape)  69.4 us
    unnamed x343, local copies, waits for them, and re-layouts  68.6 us
    all_gather x1, waiting for transfers between devices, body(): lax.all_gather(down_weight.astype(jnp.bfloat16), 'dp', axis=1, tiled=True)  44.8 us
  transfers between devices with their start and end apart: 24, of which 18 were waited for; matrix products, arithmetic and copies ran while one was open for 39% of the time, Pallas kernels for 0%

commit v1 on v0

--- a/solution.py
+++ b/solution.py
@@ -6,6 +6,18 @@
 
 HD = 128
 RATES = (0.03, 0.06, 0.02, 0.01)
+
+
+def collect(value, axis, dim):
+    ways, here, lap = (lax.axis_size(axis), lax.axis_index(axis), value.shape[dim])
+    line, have = (value, 1)
+    while have < ways:
+        line = jnp.concatenate(
+            [line, lax.ppermute(line, axis, [(d, (d - have) % ways) for d in range(ways)])],
+            axis=dim,
+        )
+        have = 2 * have
+    return jnp.roll(line, here * lap, axis=dim)
 
 
 def inverse_order(order):
@@ -151,7 +163,7 @@
     down_second,
 ):
     fetched = (
-        lax.all_gather(qkv_weight.astype(jnp.bfloat16), "dp", axis=1, tiled=True),
+        collect(qkv_weight.astype(jnp.bfloat16), "dp", 1),
         lax.all_gather(out_weight.astype(jnp.bfloat16), "dp", axis=1, tiled=True),
         lax.all_gather(proj_weight.astype(jnp.bfloat16), "dp", axis=1, tiled=True),
         lax.all_gather(down_weight.astype(jnp.bfloat16), "dp", axis=1, tiled=True),

time: 1730 us -> 1710 us (0.988)
  waiting for transfers between devices: 872 us -> 827 us
    all_gather x1 -> x0, waiting for transfers between devices: 38.6 us -> none  [body(): lax.all_gather(qkv_weight.astype(jnp.bfloat16), 'dp', axis=1, tiled=True)]
    all_gather x4, waiting for transfers between devices: 205 us -> 178 us  [gather_normed(): return lax.all_gather(rows, 'tensor', axis=0, tiled=True)]
    unnamed x343 -> x353, local copies, waits for them, and re-layouts: 68.6 us -> 73.5 us
  transfers between devices with their start and end apart: 24 -> 25, of which waited for: 18 -> 19; matrix products, arithmetic and copies ran while one was open for 39% -> 41% of each run, Pallas kernels for 0% -> 0%
where the time goes in v1:
time: 1710 us; the launch traced here: 1700 us
  waiting for transfers between devices  827 us (48%)
  local copies, waits for them, and re-layouts  363 us (21%)
  matrix products  330 us (19%)
  other arithmetic  154 us (9%)
    reduce_scatter x4, waiting for transfers between devices, sum_inputs(): lax.psum_scatter(partial_rows.astype(jnp.bfloat16), 'tensor', scatter_dim...  258 us
    all_gather x4, waiting for transfers between devices, gather_normed(): return lax.all_gather(rows, 'tensor', axis=0, tiled=True)  178 us
    reduce_scatter x4, waiting for transfers between devices, sum_branch(): lax.psum_scatter(partial_rows.astype(jnp.bfloat16), 'tensor', scatter_dim...  165 us
    all_gather x4, waiting for transfers between devices, gather_grads(): return lax.all_gather(rows, 'tensor', axis=0, tiled=True)  73.5 us
    unnamed x353, local copies, waits for them, and re-layouts  73.5 us
    all_gather x1, waiting for transfers between devices, body(): lax.all_gather(proj_weight.astype(jnp.bfloat16), 'dp', axis=1, tiled=True)  73 us
    gather x17, local copies, waits for them, and re-layouts, reorder_blocks(): return jnp.take(weight.reshape(split), order, axis=1).reshape(shape)  69.5 us
    all_gather x1, waiting for transfers between devices, body(): lax.all_gather(down_weight.astype(jnp.bfloat16), 'dp', axis=1, tiled=True)  44.8 us
  transfers between devices with their start and end apart: 25, of which 19 were waited for; matrix products, arithmetic and copies ran while one was open for 41% of the time, Pallas kernels for 0%

profile of v1, /device:TPU:0, one launch (start us, length us, event | category | flops | bytes accessed | tf_op | source)
XLA Modules:
  0.0 1699.2 jit_solution(18264029920906282923)
XLA Ops:
  101.5 25.8 %all-gather.14.cloned.1.call-done = bf16[1536,2048]{1,0:T(8,128)(2,1)} async-done(((bf16[192,2048]{1,0:T(8,128)(2,1)}), bf16[1536,2048]{1,0:T(8,128)(2,1)}) %all-gather.14.cloned.1.call-update) | async-done | bytes 6291472 | tf_op jit(solution)/shard_map/all_gather | solution.py:91
  127.3 16.3 gather_fusion.1
  187.2 16.3 gather_fusion.3
  210.5 61.5 %reduce-scatter.13.cloned.1.call-done = bf16[192,2048]{1,0:T(8,128)(2,1)} async-done(((bf16[1536,2048]{1,0:T(8,128)(2,1)}), bf16[192,2048]{1,0:T(8,128)(2,1)}) %reduce-scatter.13.cloned.1.call-update) | async-done | bytes 786448 | tf_op jit(solution)/shard_map/reduce_scatter | solution.py:99
  280.4 44.8 %all-gather.22.cloned.1.call-done = bf16[1024,2048]{1,0:T(8,128)(2,1)} async-done(((bf16[1024,512]{1,0:T(8,128)(2,1)}), bf16[1024,2048]{1,0:T(8,128)(2,1)}) %all-gather.22.cloned.1.call-update) | async-done | bytes 4194320 | tf_op jit(solution)/shard_map/all_gather | solution.py:169
  342.0 73.0 %all-gather.18.cloned.1.call-done = bf16[2,2048,1024]{2,1,0:T(8,128)(2,1)} async-done(((bf16[2,512,1024]{2,1,0:T(8,128)(2,1)}), bf16[2,2048,1024]{2,1,0:T(8,128)(2,1)}) %all-gather.18.cloned.1.call-update) | async-done | bytes 8388624 | tf_op jit(solution)/shard_map/all_gather | solution.py:168
  454.3 27.4 %all-gather.20.cloned.1.call-done = bf16[1536,2048]{1,0:T(8,128)(2,1)} async-done(((bf16[192,2048]{1,0:T(8,128)(2,1)}), bf16[1536,2048]{1,0:T(8,128)(2,1)}) %all-gather.20.cloned.1.call-update) | async-done | bytes 6291472 | tf_op jit(solution)/shard_map/all_gather | solution.py:91
  481.8 19.2 %convolution_bitcast_fusion.3 = f32[2,1536,1024]{1,2,0:T(8,128)} fusion(bf16[2,2048,1024]{2,1,0:T(8,128)(2,1)} %bitcast_select_fusion.1, bf16[1536,2048]{1,0:T(8,128)(2,1)} %all-gather.20.cloned.1.call-done), kind=kOutput, calls=%fused_computation.38 | convolution fusion | flops 12884901888 | bytes 27262976 | tf_op jit(solution)/shard_map/td,sdf->stf/dot_general | solution.py:230
  519.4 27.3 %all-gather.32.cloned.1.call-done = bf16[1,1536,2048]{2,1,0:T(8,128)(2,1)} async-done(((bf16[1,192,2048]{2,1,0:T(8,128)(2,1)}), bf16[1,1536,2048]{2,1,0:T(8,128)(2,1)}) %all-gather.32.cloned.1.call-update) | async-done | bytes 6291472 | tf_op jit(solution)/shard_map/all_gather | solution.py:95
  546.8 14.9 fusion.71
  564.3 17.7 %bitcast_convert_fusion.1 = bf16[1536,2048]{1,0:T(8,128)(2,1)} fusion(bf16[2,2048,1024]{2,1,0:T(8,128)(2,1)} %bitcast_select_fusion.1, bf16[1,1536,1024]{1,2,0:T(8,128)(2,1)S(1)} %get-tuple-element.268, bf16[1,1536,1024]{1,2,0:T(8,128)(2,1)S(1)} %get-tuple-element.267), kind=kOutput, calls=%fused_computation.29 | convolution fusion | flops 12891193344 | bytes 20971520 | tf_op jit(solution)/shard_map/stf,sdf->td/dot_general | solution.py:247
  582.7 34.8 %reduce-scatter.15.cloned.1.call-done = bf16[192,2048]{1,0:T(8,128)(2,1)} async-done(((bf16[1536,2048]{1,0:T(8,128)(2,1)}), bf16[192,2048]{1,0:T(8,128)(2,1)}) %reduce-scatter.15.cloned.1.call-update) | async-done | bytes 786448 | tf_op jit(solution)/shard_map/reduce_scatter | solution.py:99
  617.5 70.5 %reduce-scatter.21.cloned.1.call-done = bf16[192,2048]{1,0:T(8,128)(2,1)} async-done(((bf16[1536,2048]{1,0:T(8,128)(2,1)}), bf16[192,2048]{1,0:T(8,128)(2,1)}) %reduce-scatter.21.cloned.1.call-update) | async-done | bytes 786448 | tf_op jit(solution)/shard_map/reduce_scatter | solution.py:105
  694.7 62.5 %all-gather.24.cloned.1.call-done = bf16[1536,2048]{1,0:T(8,128)(2,1)} async-done(((bf16[192,2048]{1,0:T(8,128)(2,1)}), bf16[1536,2048]{1,0:T(8,128)(2,1)}) %all-gather.24.cloned.1.call-update) | async-done | bytes 6291472 | tf_op jit(solution)/shard_map/all_gather | solution.py:91
  757.2 16.3 gather_fusion.5
  811.6 16.3 gather_fusion.6
  830.5 17.1 %gather_fusion.7 = bf16[1536,2048]{1,0:T(8,128)(2,1)} fusion(bf16[1536,2048]{1,0:T(8,128)(2,1)} %all-gather.28.cloned.1.call-done, s32[2048]{0:T(1024)S(1)} %copy-done.87), kind=kCustom, calls=%fused_computation.7 | custom fusion | bytes 12589056 | tf_op jit(solution)/shard_map/gather | solution.py:250
  890.2 16.4 gather_fusion.8
  906.7 68.0 %reduce-scatter.23.cloned.1.call-done = bf16[192,2048]{1,0:T(8,128)(2,1)} async-done(((bf16[1536,2048]{1,0:T(8,128)(2,1)}), bf16[192,2048]{1,0:T(8,128)(2,1)}) %reduce-scatter.23.cloned.1.call-update) | async-done | bytes 786448 | tf_op jit(solution)/shard_map/reduce_scatter | solution.py:105
  979.6 62.7 %all-gather.26.cloned.1.call-done = bf16[1536,2048]{1,0:T(8,128)(2,1)} async-done(((bf16[192,2048]{1,0:T(8,128)(2,1)}), bf16[1536,2048]{1,0:T(8,128)(2,1)}) %all-gather.26.cloned.1.call-update) | async-done | bytes 6291472 | tf_op jit(solution)/shard_map/all_gather | solution.py:91
  1042.3 19.2 %convolution_bitcast_fusion.2 = f32[2,1536,1024]{1,2,0:T(8,128)} fusion(bf16[2,2048,1024]{2,1,0:T(8,128)(2,1)} %bitcast_select_fusion.1, bf16[1536,2048]{1,0:T(8,128)(2,1)} %all-gather.26.cloned.1.call-done), kind=kOutput, calls=%fused_computation.37 | convolution fusion | flops 12884901888 | bytes 27262976 | tf_op jit(solution)/shard_map/td,sdf->stf/dot_general | solution.py:230
  1061.5 46.2 %all-gather.34.cloned.1.call-done = bf16[1,1536,2048]{2,1,0:T(8,128)(2,1)} async-done(((bf16[1,192,2048]{2,1,0:T(8,128)(2,1)}), bf16[1,1536,2048]{2,1,0:T(8,128)(2,1)}) %all-gather.34.cloned.1.call-update) | async-done | bytes 6291472 | tf_op jit(solution)/shard_map/all_gather | solution.py:95
  1107.7 15.1 fusion.72
  1125.4 17.8 %bitcast_convert_fusion = bf16[1536,2048]{1,0:T(8,128)(2,1)} fusion(bf16[2,2048,1024]{2,1,0:T(8,128)(2,1)} %bitcast_select_fusion.1, bf16[1,1536,1024]{1,2,0:T(8,128)(2,1)S(1)} %get-tuple-element.266, bf16[1,1536,1024]{1,2,0:T(8,128)(2,1)S(1)} %get-tuple-element.265), kind=kOutput, calls=%fused_computation.28 | convolution fusion | flops 12891193344 | bytes 20971520 | tf_op jit(solution)/shard_map/stf,sdf->td/dot_general | solution.py:247
  1143.3 15.1 convolution_convert_fusion
  1158.9 52.9 %reduce-scatter.25.cloned.1.call-done = bf16[192,2048]{1,0:T(8,128)(2,1)} async-done(((bf16[1536,2048]{1,0:T(8,128)(2,1)}), bf16[192,2048]{1,0:T(8,128)(2,1)}) %reduce-scatter.25.cloned.1.call-update) | async-done | bytes 786448 | tf_op jit(solution)/shard_map/reduce_scatter | solution.py:105
  1213.7 68.5 %reduce-scatter.19.cloned.1.call-done = bf16[192,2048]{1,0:T(8,128)(2,1)} async-done(((bf16[1536,2048]{1,0:T(8,128)(2,1)}), bf16[192,2048]{1,0:T(8,128)(2,1)}) %reduce-scatter.19.cloned.1.call-update) | async-done | bytes 786448 | tf_op jit(solution)/shard_map/reduce_scatter | solution.py:99
  1336.7 19.7 %fusion.34 = f32[2,1024,2048]{2,1,0:T(8,128)} fusion(bf16[1536,2048]{1,0:T(8,128)(2,1)} %all-gather.20.cloned.1.call-done, bf16[1,1536,1024]{1,2,0:T(8,128)(2,1)} %copy-done.152, bf16[1,1536,1024]{1,2,0:T(8,128)(2,1)S(1)} %copy-done.151), kind=kOutput, calls=%fused_computation.87 | convolution fusion | flops 12888047616 | bytes 29360128 | tf_op jit(solution)/shard_map/td,stf->sdf/dot_general | solution.py:243
  1356.4 22.3 %add_bitcast_fusion = bf16[2,2048,1024]{1,2,0:T(8,128)(2,1)} fusion(f32[2,1024,2048]{2,1,0:T(8,128)} %fusion.34, bf16[1536,2048]{1,0:T(8,128)(2,1)} %all-gather.26.cloned.1.call-done, bf16[1,1536,1024]{1,2,0:T(8,128)(2,1)} %copy-done.154, bf16[1,1536,1024]{1,2,0:T(8,128)(2,1)} %copy-done.153), kind=kOutput, calls=%fused_computation.27 | convolution fusion | flops 12896436224 | bytes 37748736 | tf_op jit(solution)/shard_map/td,stf->sdf/dot_general | solution.py:243
  1457.5 16.4 gather_fusion.9
  1558.6 16.4 gather_fusion.10
  1619.5 66.4 %reduce-scatter.27.cloned.1.call-done = bf16[192,2048]{1,0:T(8,128)(2,1)} async-done(((bf16[1536,2048]{1,0:T(8,128)(2,1)}), bf16[192,2048]{1,0:T(8,128)(2,1)}) %reduce-scatter.27.cloned.1.call-update) | async-done | bytes 786448 | tf_op jit(solution)/shard_map/reduce_scatter | solution.py:105
  (650 shorter events, 597.6 us)
Async XLA Ops:
  7.2 53.1 %all-gather.16.cloned.1.call-start = ((), (), s32[]{:S(2)}) async-start(), calls=%async_computation.13 | async-start | bytes 1310720 | tf_op jit(solution)/shard_map/all_gather | solution.py:167
  9.5 117.8 %all-gather.14.cloned.1.call-start = ((), (), s32[]{:S(2)}) async-start(), calls=%async_computation.12 | async-start | bytes 7077888 | tf_op jit(solution)/shard_map/all_gather | solution.py:91
  12.8 259.2 %reduce-scatter.13.cloned.1.call-start = ((), (), s32[]{:S(2)}) async-start(), calls=%async_computation.14 | async-start | bytes 7077888 | tf_op jit(solution)/shard_map/reduce_scatter | solution.py:99
  15.3 23.5 %collective-permute-start = (bf16[3,512,256]{2,1,0:T(8,128)(2,1)S(1)}, bf16[3,512,256]{2,1,0:T(8,128)(2,1)S(1)}, u32[]{:S(2)}, u32[]{:S(2)}) collective-permute-start(bf16[3,512,256]{2,1,0:T(8,128)(2,1)S(1)} %get-tuple-element.264), channel_id=1, source_target_pairs={{0,24},{8,0},{16,8},{24,16},{1,25},{9,1},{17,9},{25,17},{2,26},{10... | collective-permute-start | bytes 2359304 | tf_op jit(solution)/shard_map/ppermute | solution.py:16
  19.8 259.4 %copy-start.146 = (s32[4]{0:T(128)}, s32[4]{0:T(128)S(1)}, u32[]{:S(2)}) copy-start(s32[4]{0:T(128)S(1)} %get-tuple-element.330) | copy-start | bytes 52
  34.7 92.5 %copy-start.86 = (s32[2048]{0:T(1024)}, s32[2048]{0:T(1024)S(1)}, u32[]{:S(2)}) copy-start(s32[2048]{0:T(1024)S(1)} %pad_clamp_fusion.3) | copy-start | bytes 24580
  35.4 151.7 %copy-start.92 = (s32[2048]{0:T(1024)}, s32[2048]{0:T(1024)S(1)}, u32[]{:S(2)}) copy-start(s32[2048]{0:T(1024)S(1)} %get-tuple-element.370) | copy-start | bytes 24580
  40.1 41.7 %collective-permute-start.1 = (bf16[3,1024,256]{2,1,0:T(8,128)(2,1)}, bf16[3,1024,256]{2,1,0:T(8,128)(2,1)}, u32[]{:S(2)}, u32[]{:S(2)}) collective-permute-start(bf16[3,1024,256]{2,1,0:T(8,128)(2,1)} %pad_maximum_fusion.9), channel_id=1, source_target_pairs={{0,16},{8,24},{16,0},{24,8},{1,17},{9,25},{17,1},{25,9},{2,18},{10... | collective-permute-start | bytes 4718600 | tf_op jit(solution)/shard_map/ppermute | solution.py:16
  68.0 114.3 %copy-start.31 = (bf16[256,4,512]{0,2,1:T(8,128)(2,1)}, bf16[256,4,512]{0,2,1:T(8,128)(2,1)S(1)}, u32[]{:S(2)}) copy-start(bf16[256,4,512]{0,2,1:T(8,128)(2,1)S(1)} %copy.216) | copy-start | bytes 3145732
  203.5 121.7 %all-gather.22.cloned.1.call-start = ((), (), s32[]{:S(2)}) async-start(), calls=%async_computation.17 | async-start | bytes 5242880 | tf_op jit(solution)/shard_map/all_gather | solution.py:169
  206.2 208.7 %all-gather.18.cloned.1.call-start = ((), (), s32[]{:S(2)}) async-start(), calls=%async_computation.15 | async-start | bytes 10485760 | tf_op jit(solution)/shard_map/all_gather | solution.py:168
  210.5 271.3 %all-gather.20.cloned.1.call-start = ((), (), s32[]{:S(2)}) async-start(), calls=%async_computation.16 | async-start | bytes 7077888 | tf_op jit(solution)/shard_map/all_gather | solution.py:91
  276.3 270.5 %all-gather.32.cloned.1.call-start = ((), (), s32[]{:S(2)}) async-start(), calls=%async_computation.33 | async-start | bytes 7077888 | tf_op jit(solution)/shard_map/all_gather | solution.py:95
  279.1 338.4 %reduce-scatter.15.cloned.1.call-start = ((), (), s32[]{:S(2)}) async-start(), calls=%async_computation.18 | async-start | bytes 7077888 | tf_op jit(solution)/shard_map/reduce_scatter | solution.py:99
  515.3 172.7 %reduce-scatter.21.cloned.1.call-start = ((), (), s32[]{:S(2)}) async-start(), calls=%async_computation.23 | async-start | bytes 7077888 | tf_op jit(solution)/shard_map/reduce_scatter | solution.py:105
  582.1 175.2 %all-gather.24.cloned.1.call-start = ((), (), s32[]{:S(2)}) async-start(), calls=%async_computation.19 | async-start | bytes 7077888 | tf_op jit(solution)/shard_map/all_gather | solution.py:91
  582.7 111.2 %copy-start.111 = (f32[192]{0:T(256)}, f32[192]{0:T(256)S(1)}, u32[]{:S(2)}) copy-start(f32[192]{0:T(256)S(1)} %broadcast_multiply_fusion.9) | copy-start | bytes 2308
  693.9 136.6 %all-gather.28.cloned.1.call-start = ((), (), s32[]{:S(2)}) async-start(), calls=%async_computation.24 | async-start | bytes 7077888 | tf_op jit(solution)/shard_map/all_gather | solution.py:95
  694.7 212.0 %reduce-scatter.17.cloned.1.call-start = ((), (), s32[]{:S(2)}) async-start(), calls=%async_computation.20 | async-start | bytes 7077888 | tf_op jit(solution)/shard_map/reduce_scatter | solution.py:99
  828.0 146.6 %reduce-scatter.23.cloned.1.call-start = ((), (), s32[]{:S(2)}) async-start(), calls=%async_computation.25 | async-start | bytes 7077888 | tf_op jit(solution)/shard_map/reduce_scatter | solution.py:105
  906.6 135.7 %all-gather.26.cloned.1.call-start = ((), (), s32[]{:S(2)}) async-start(), calls=%async_computation.21 | async-start | bytes 7077888 | tf_op jit(solution)/shard_map/all_gather | solution.py:91
  979.0 128.8 %all-gather.34.cloned.1.call-start = ((), (), s32[]{:S(2)}) async-start(), calls=%async_computation.34 | async-start | bytes 7077888 | tf_op jit(solution)/shard_map/all_gather | solution.py:95
  979.5 232.2 %reduce-scatter.25.cloned.1.call-start = ((), (), s32[]{:S(2)}) async-start(), calls=%async_computation.26 | async-start | bytes 7077888 | tf_op jit(solution)/shard_map/reduce_scatter | solution.py:105
  1143.3 138.9 %reduce-scatter.19.cloned.1.call-start = ((), (), s32[]{:S(2)}) async-start(), calls=%async_computation.22 | async-start | bytes 7077888 | tf_op jit(solution)/shard_map/reduce_scatter | solution.py:99
  1158.5 299.0 %all-gather.30.cloned.1.call-start = ((), (), s32[]{:S(2)}) async-start(), calls=%async_computation.27 | async-start | bytes 7077888 | tf_op jit(solution)/shard_map/all_gather | solution.py:95
  1286.4 292.0 %reduce-scatter.35.cloned.1.call-start = ((), (), s32[]{:S(2)}) async-start(), calls=%async_computation.32 | async-start | bytes 5242880 | tf_op jit(solution)/shard_map/reduce_scatter | solution.py:130
  1334.8 251.6 %reduce-scatter.33.cloned.1.call-start = ((), (), s32[]{:S(2)}) async-start(), calls=%async_computation.31 | async-start | bytes 10485760 | tf_op jit(solution)/shard_map/reduce_scatter | solution.py:124
  1450.5 146.7 %reduce-scatter.31.cloned.1.call-start = ((), (), s32[]{:S(2)}) async-start(), calls=%async_computation.30 | async-start | bytes 1310720 | tf_op jit(solution)/shard_map/reduce_scatter | solution.py:118
  1520.1 93.7 %reduce-scatter.29.cloned.1.call-start = ((), (), s32[]{:S(2)}) async-start(), calls=%async_computation.29 | async-start | bytes 3932160 | tf_op jit(solution)/shard_map/reduce_scatter | solution.py:112
  1547.7 138.2 %reduce-scatter.27.cloned.1.call-start = ((), (), s32[]{:S(2)}) async-start(), calls=%async_computation.28 | async-start | bytes 7077888 | tf_op jit(solution)/shard_map/reduce_scatter | solution.py:105
  1602.6 85.1 %copy-start.110 = (f32[192]{0:T(256)S(1)}, f32[192]{0:T(256)}, u32[]{:S(2)}) copy-start(f32[192]{0:T(256)} %copy-done.108) | copy-start | bytes 2308
  1602.6 85.1 %copy-start.127 = (f32[192]{0:T(256)S(1)}, f32[192]{0:T(256)}, u32[]{:S(2)}) copy-start(f32[192]{0:T(256)} %copy-done.125) | copy-start | bytes 2308
  (154 other events, 1635.8 us)
Sparse Core Ops, SparseCore 0:
  10.4 49.8 all-gather.15
  62.5 64.6 all-gather.13
  203.6 68.3 reduce-scatter.12
  274.3 50.8 all-gather.21
  327.4 87.4 all-gather.17
  417.0 64.6 all-gather.19
  483.4 63.3 all-gather.31
  549.1 68.3 reduce-scatter.14
  619.8 68.1 reduce-scatter.20
  694.0 63.1 all-gather.23
  759.4 63.3 all-gather.27
  828.1 68.4 reduce-scatter.16
  906.7 67.8 reduce-scatter.22
  979.1 63.1 all-gather.25
  1044.3 63.3 all-gather.33
  1143.4 68.3 reduce-scatter.24
  1213.9 68.1 reduce-scatter.18
  1286.6 63.1 all-gather.29
  1352.7 51.2 reduce-scatter.34
  1450.6 84.8 reduce-scatter.32
  1539.0 27.9 reduce-scatter.30
  1569.9 43.8 reduce-scatter.28
  1616.2 69.7 reduce-scatter.26
